TPU v7x, 512 devices: a whole 4x4x16 slice. The times are simulated.
512 devices in a mesh: ep: 64 (over x_lo, z, core), blk: 8 (over x_hi, y).
Axes of the slice: x: 4 (x_hi: 2, x_lo: 2; x = x_hi * 2 + x_lo), y: 4, z: 16, core: 2. Of those that a mesh axis runs over, the one named last changes fastest.
Arguments:
- tokens: bfloat16 [4096, 2048], P(('ep', 'blk')), may hold values from -6 to 6
- routes: int32 [4096, 8], P('ep'), may hold values from 0 to 63, all different within a row; in each aligned block of 64 rows (0 to 63, 64 to 127, ...) at most 16 rows name the same one
- gate_scale: bfloat16 [4096, 8], P('ep'), may hold values from 0.099609375 to 1
- placement: int32 [64], replicated, may hold values from 0 to 63, each once
- w_gate: bfloat16 [64, 2048, 1024], P('ep', None, 'blk'), may hold values from -0.125 to 0.125
- w_up: bfloat16 [64, 2048, 1024], P('ep', None, 'blk'), may hold values from -0.125 to 0.125
- w_down: bfloat16 [64, 1024, 2048], P('ep', 'blk'), may hold values from -0.1875 to 0.1875
Outputs:
- mixed: bfloat16 [4096, 2048], P(('ep', 'blk'))
Inputs may be any that keep to these rules, and one draw needn't show every extreme that they name: `routes`: in each aligned block of 64 rows (the tokens of one index of ep) no expert is named by more than 16 rows, a bound that some block reaches; a row names 8 different experts. `placement`: each ep index holds exactly one expert.
All inputs are finite; a program needn't handle non-finite values.
Results may differ from a plain program's by a relative error of at most 0.019.
Values may be sent and summed in bfloat16 or wider, within the bound.
A program may use at most 64 MiB of HBM per device.

v0:
```python
import jax
import jax.numpy as jnp
from jax import lax
from jax.sharding import Mesh, PartitionSpec as P

AXES = ("xl", "z", "core", "xh", "y")
EP = ("xl", "z", "core")
BLK = ("xh", "y")
PLANE = ("y", "xh", "xl", "z")


def local(tokens, routes, gate_scale, placement, w_gate, w_up, w_down):
    own = tokens.shape[0]
    experts = placement.shape[0]
    blk_index = lax.axis_index("xh") * lax.axis_size("y") + lax.axis_index("y")
    my_routes = lax.dynamic_slice_in_dim(routes, blk_index * own, own, 0)
    my_scale = lax.dynamic_slice_in_dim(gate_scale, blk_index * own, own, 0)
    ids = lax.iota(jnp.int32, experts)
    chosen = my_routes[:, :, None] == ids[None, None, :]
    holder = jnp.sum(jnp.where(chosen, placement[None, None, :], 0), axis=-1)
    dense = jnp.sum(
        jnp.where(
            holder[:, :, None] == ids[None, None, :], my_scale[:, :, None].astype(jnp.float32), 0.0
        ),
        axis=1,
    ).astype(jnp.bfloat16)
    packed = jnp.concatenate([tokens, dense, jnp.zeros_like(dense)], axis=1)
    everyone = lax.all_gather(packed, "z", axis=0, tiled=True)
    everyone = lax.all_gather(everyone, ("xh", "xl"), axis=0, tiled=True)
    everyone = lax.all_gather(everyone, "y", axis=0, tiled=True)
    width = tokens.shape[1]
    x = everyone[:, :width]
    weights = everyone[:, width : width + experts]
    swap = [(0, 1), (1, 0)]
    wg = jnp.concatenate([w_gate[0], lax.ppermute(w_gate[0], "core", swap)], axis=1)
    wu = jnp.concatenate([w_up[0], lax.ppermute(w_up[0], "core", swap)], axis=1)
    wd = jnp.concatenate([w_down[0], lax.ppermute(w_down[0], "core", swap)], axis=0)
    core = lax.axis_index("core")
    pair = (lax.axis_index("xl") * lax.axis_size("z") + lax.axis_index("z")) * 2
    mine = lax.dynamic_slice_in_dim(weights, pair + core, 1, 1).astype(jnp.float32)
    other = lax.dynamic_slice_in_dim(weights, pair + 1 - core, 1, 1).astype(jnp.float32)
    half = w_down.shape[1]
    first = lax.broadcasted_iota(jnp.int32, (1, 2 * half), 1) < half
    scale = jnp.where(first, mine, other)
    gate = jnp.dot(x, wg, preferred_element_type=jnp.float32)
    up = jnp.dot(x, wu, preferred_element_type=jnp.float32)
    hidden = (jax.nn.silu(gate) * up * scale).astype(jnp.bfloat16)
    out = jnp.dot(hidden, wd, preferred_element_type=jnp.float32).astype(jnp.bfloat16)
    part = lax.psum_scatter(out, "y", scatter_dimension=0, tiled=True)
    part = lax.optimization_barrier(
        lax.psum_scatter(part, ("xh", "xl"), scatter_dimension=0, tiled=True).astype(jnp.float32)
    )
    total = lax.psum_scatter(part, "z", scatter_dimension=0, tiled=True)
    return lax.optimization_barrier(total).astype(jnp.bfloat16)


def solution(mesh):
    fine = Mesh(mesh.devices.reshape(2, 16, 2, 2, 4), AXES)
    in_specs = (
        P(AXES, None),
        P(EP, None),
        P(EP, None),
        P(),
        P(EP, None, BLK),
        P(EP, None, BLK),
        P(EP, BLK, None),
    )
    return jax.shard_map(
        local, mesh=fine, in_specs=in_specs, out_specs=P(AXES, None), check_vma=False
    )
```

profile of v0, /device:TPU:6, one launch (start us, length us, event | category | flops | bytes accessed | tf_op | source)
XLA Modules:
  0.0 417.5 jit_solution(12385986493303225261)
XLA Ops:
  6.5 0.0 all-gather.3.cloned.1.call-start
  6.6 0.6 copy-done
  7.2 0.1 constant_dynamic-slice_fusion
  7.3 0.1 copy.12
  7.4 0.8 dynamic-slice_convert_fusion
  8.1 0.1 copy.13
  8.2 0.9 select_reduce_fusion.1
  9.1 0.1 select_reduce_fusion
  9.2 0.8 concatenate.12
  10.1 40.7 %all_gather.9 = bf16[128,2176]{1,0:T(8,128)(2,1)} all-gather(bf16[8,2176]{1,0:T(8,128)(2,1)S(1)} %concatenate.12), channel_id=1, replica_groups=mesh['xl'=2,'z'=16,'core'=2,'xh'=2,'y'=4] {'z'}, dimensions={0}, use_global_device_ids=true | all-gather | bytes 591872 | tf_op jit(solution)/shard_map/all_gather | solution.py:28
  50.8 0.0 all-gather.3.cloned.1.call-update
  50.8 0.0 all-gather.5.cloned.1.call-start
  50.8 34.0 %all-gather.3.cloned.1.call-done = bf16[512,2176]{1,0:T(8,128)(2,1)} async-done(((bf16[128,2176]{1,0:T(8,128)(2,1)}), bf16[512,2176]{1,0:T(8,128)(2,1)}) %all-gather.3.cloned.1.call-update) | async-done | bytes 2228240 | tf_op jit(solution)/shard_map/all_gather | solution.py:29
  84.9 0.0 all-gather.5.cloned.1.call-update
  84.9 0.0 reduce-scatter.4.cloned.1.call-start
  84.9 1.9 collective-permute-start.1
  86.9 2.4 collective-permute-start
  89.3 1.9 collective-permute-start.2
  91.3 92.9 %all-gather.5.cloned.1.call-done = bf16[2048,2176]{1,0:T(8,128)(2,1)} async-done(((bf16[512,2176]{1,0:T(8,128)(2,1)}), bf16[2048,2176]{1,0:T(8,128)(2,1)}) %all-gather.5.cloned.1.call-update) | async-done | bytes 8912912 | tf_op jit(solution)/shard_map/all_gather | solution.py:30
  184.1 1.1 slice.9
  185.2 0.7 convert_reduce_fusion.1
  186.0 7.1 %fusion = f32[2048,256]{1,0:T(8,128)} fusion(bf16[2048,2176]{1,0:T(8,128)(2,1)} %all-gather.5.cloned.1.call-done, bf16[2048,128]{1,0:T(8,128)(2,1)S(1)} %collective-permute-done.1, bf16[2048,128]{1,0:T(8,128)(2,1)S(1)} %bitcast.4), kind=kOutput, calls=%fused_computation.1 | convolution fusion | flops 2149580800 | bytes 11534336 | tf_op jit(solution)/shard_map/dot_general | solution.py:46
  193.1 13.3 %convolution_convert_fusion = bf16[2048,2048]{1,0:T(8,128)(2,1)} fusion(f32[2048,256]{1,0:T(8,128)} %fusion, bf16[128,2048]{1,0:T(8,128)(2,1)S(1)} %collective-permute-done.2, bf16[128,2048]{1,0:T(8,128)(2,1)S(1)} %bitcast.6, f32[2048]{0:T(1024)S(1)} %get-tuple-element.6, f32[2048]{0:T(1024)S(1)} %get-tuple-element.5, ...), kind=kOutput, calls=%fused_computation | convolution fusion | flops 4307550208 | bytes 20988160 | tf_op jit(solution)/shard_map/dot_general | solution.py:48
  206.3 0.0 reduce-scatter.4.cloned.1.call-update
  206.3 0.0 reduce-scatter.6.cloned.1.call-start
  206.4 89.4 %reduce-scatter.4.cloned.1.call-done = bf16[512,2048]{1,0:T(8,128)(2,1)} async-done(((bf16[2048,2048]{1,0:T(8,128)(2,1)}), bf16[512,2048]{1,0:T(8,128)(2,1)}) %reduce-scatter.4.cloned.1.call-update) | async-done | bytes 2097168 | tf_op jit(solution)/shard_map/reduce_scatter | solution.py:49
  295.8 0.0 reduce-scatter.8.cloned.1.call-start
  295.9 37.9 %reduce-scatter.6.cloned.1.call-done = bf16[128,2048]{1,0:T(8,128)(2,1)} async-done(((bf16[512,2048]{1,0:T(8,128)(2,1)}), bf16[128,2048]{1,0:T(8,128)(2,1)}) %reduce-scatter.6.cloned.1.call-update) | async-done | bytes 524304 | tf_op jit(solution)/shard_map/reduce_scatter | solution.py:51
  333.8 2.1 convert_element_type.25
  335.9 0.0 reduce-scatter.8.cloned.1.call-update
  335.9 73.6 %reduce-scatter.8.cloned.1.call-done = f32[8,2048]{1,0:T(8,128)} async-done(((f32[128,2048]{1,0:T(8,128)}), f32[8,2048]{1,0:T(8,128)}) %reduce-scatter.8.cloned.1.call-update) | async-done | bytes 65552 | tf_op jit(solution)/shard_map/reduce_scatter | solution.py:53
  409.5 1.5 convert_element_type.26
  (13 shorter events, 0.0 us)
Async XLA Ops:
  6.5 0.7 copy-start
  6.5 78.4 %copy-start.1 = (bf16[1,2048,128]{2,1,0:T(8,128)(2,1)S(1)}, bf16[1,2048,128]{2,1,0:T(8,128)(2,1)}, u32[]{:S(2)}) copy-start(bf16[1,2048,128]{2,1,0:T(8,128)(2,1)} %param.12) | copy-start | bytes 1572868
  6.5 80.3 %copy-start.3 = (bf16[1,2048,128]{2,1,0:T(8,128)(2,1)S(1)}, bf16[1,2048,128]{2,1,0:T(8,128)(2,1)}, u32[]{:S(2)}) copy-start(bf16[1,2048,128]{2,1,0:T(8,128)(2,1)} %param.11) | copy-start | bytes 1572868
  6.5 82.7 %copy-start.2 = (bf16[1,128,2048]{2,1,0:T(8,128)(2,1)S(1)}, bf16[1,128,2048]{2,1,0:T(8,128)(2,1)}, u32[]{:S(2)}) copy-start(bf16[1,128,2048]{2,1,0:T(8,128)(2,1)} %param.13) | copy-start | bytes 1572868
  6.5 78.3 %all-gather.3.cloned.1.call-start = ((), (), s32[]{:S(2)}) async-start(), calls=%async_computation.3 | async-start | bytes 2785280 | tf_op jit(solution)/shard_map/all_gather | solution.py:29
  50.8 133.3 %all-gather.5.cloned.1.call-start = ((), (), s32[]{:S(2)}) async-start(), calls=%async_computation.4 | async-start | bytes 11141120 | tf_op jit(solution)/shard_map/all_gather | solution.py:30
  84.9 210.9 %reduce-scatter.4.cloned.1.call-start = ((), (), s32[]{:S(2)}) async-start(), calls=%async_computation.5 | async-start | bytes 10485760 | tf_op jit(solution)/shard_map/reduce_scatter | solution.py:49
  84.9 101.0 %collective-permute-start.1 = (bf16[2048,128]{1,0:T(8,128)(2,1)S(1)}, bf16[2048,128]{1,0:T(8,128)(2,1)S(1)}, u32[]{:S(2)}, u32[]{:S(2)}) collective-permute-start(bf16[2048,128]{1,0:T(8,128)(2,1)S(1)} %bitcast.3), channel_id=1, source_target_pairs={{0,8},{8,0},{1,9},{9,1},{2,10},{10,2},{3,11},{11,3},{4,12},{12,4},... | collective-permute-start | bytes 1572872 | tf_op jit(solution)/shard_map/ppermute | solution.py:36
  86.9 106.2 %collective-permute-start = (bf16[2048,128]{1,0:T(8,128)(2,1)S(1)}, bf16[2048,128]{1,0:T(8,128)(2,1)S(1)}, u32[]{:S(2)}, u32[]{:S(2)}) collective-permute-start(bf16[2048,128]{1,0:T(8,128)(2,1)S(1)} %bitcast.7), channel_id=1, source_target_pairs={{0,8},{8,0},{1,9},{9,1},{2,10},{10,2},{3,11},{11,3},{4,12},{12,4},... | collective-permute-start | bytes 1572872 | tf_op jit(solution)/shard_map/ppermute | solution.py:35
  89.3 103.8 %collective-permute-start.2 = (bf16[128,2048]{1,0:T(8,128)(2,1)S(1)}, bf16[128,2048]{1,0:T(8,128)(2,1)S(1)}, u32[]{:S(2)}, u32[]{:S(2)}) collective-permute-start(bf16[128,2048]{1,0:T(8,128)(2,1)S(1)} %bitcast.5), channel_id=1, source_target_pairs={{0,8},{8,0},{1,9},{9,1},{2,10},{10,2},{3,11},{11,3},{4,12},{12,4},... | collective-permute-start | bytes 1572872 | tf_op jit(solution)/shard_map/ppermute | solution.py:37
  206.3 127.5 %reduce-scatter.6.cloned.1.call-start = ((), (), s32[]{:S(2)}) async-start(), calls=%async_computation.6 | async-start | bytes 2621440 | tf_op jit(solution)/shard_map/reduce_scatter | solution.py:51
  295.8 113.7 %reduce-scatter.8.cloned.1.call-start = ((), (), s32[]{:S(2)}) async-start(), calls=%async_computation.7 | async-start | bytes 1114112 | tf_op jit(solution)/shard_map/reduce_scatter | solution.py:53
Sparse Core Ops, SparseCore 0:
  50.9 33.8 all-gather.2
  86.9 97.1 all-gather.4
  206.5 89.2 reduce-scatter.3
  298.5 35.2 reduce-scatter.5
  336.5 73.0 reduce-scatter.7
where the time goes:
time: 418 us
  waiting for transfers between devices  328 us (78%)
  blocking collectives  40.7 us (10%)
  matrix products  20.4 us (5%)
  between operations  13.3 us (3%)
  starting transfers between devices  6.44 us (2%)
  other arithmetic  6.1 us (1%)
    all_gather x1, waiting for transfers between devices, local(): everyone = lax.all_gather(everyone, 'y', axis=0, tiled=True)  92.9 us
    reduce_scatter x1, waiting for transfers between devices, local(): part = lax.psum_scatter(out, 'y', scatter_dimension=0, tiled=True)  89.4 us
    reduce_scatter x1, waiting for transfers between devices, local(): total = lax.psum_scatter(part, 'z', scatter_dimension=0, tiled=True)  73.6 us
    all_gather x1, blocking collectives, local(): everyone = lax.all_gather(packed, 'z', axis=0, tiled=True)  40.7 us
    reduce_scatter x1, waiting for transfers between devices, local(): lax.psum_scatter(part, ('xh', 'xl'), scatter_dimension=0, tiled=True)  37.9 us
    all_gather x1, waiting for transfers between devices, local(): everyone = lax.all_gather(everyone, ('xh', 'xl'), axis=0, tiled=True)  34 us
    dot_general x1, matrix products, local(): jnp.dot(hidden, wd, preferred_element_type=jnp.float32).astype(jnp.bfloat16)  13.3 us
  transfers between devices with their start and end apart: 8, of which 5 were waited for; matrix products, arithmetic and copies ran while one was open for 2% of the time, Pallas kernels for 0%

commit v1 on v0

--- a/solution.py
+++ b/solution.py
@@ -26,7 +26,15 @@
     ).astype(jnp.bfloat16)
     packed = jnp.concatenate([tokens, dense, jnp.zeros_like(dense)], axis=1)
     everyone = lax.all_gather(packed, "z", axis=0, tiled=True)
-    everyone = lax.all_gather(everyone, ("xh", "xl"), axis=0, tiled=True)
+    everyone = jnp.concatenate(
+        lax.all_to_all(
+            jnp.stack(lax.psum(1, axis_name=("xh", "xl")) * [everyone], 0),
+            axis_name=("xh", "xl"),
+            split_axis=0,
+            concat_axis=0,
+        ),
+        0,
+    )
     everyone = lax.all_gather(everyone, "y", axis=0, tiled=True)
     width = tokens.shape[1]
     x = everyone[:, :width]

time: 418 us -> 400 us (0.957)
  waiting for transfers between devices: 328 us -> 285 us
  blocking collectives: 40.7 us -> 61.4 us
  local copies, waits for them, and re-layouts: 2.78 us -> 7.15 us
    all_gather x1 -> x0, waiting for transfers between devices: 34 us -> none  [local(): everyone = lax.all_gather(everyone, ('xh', 'xl'), axis=0, tiled=True)]
    all_to_all x0 -> x1, blocking collectives: none -> 22.7 us  [local(): lax.all_to_all(jnp.stack(lax.psum(1, axis_name=('xh', 'xl')) * [everyone]...]
    all_gather x1, waiting for transfers between devices: 92.9 us -> 84.2 us  [local(): everyone = lax.all_gather(everyone, 'y', axis=0, tiled=True)]
  transfers between devices with their start and end apart: 8 -> 7, of which waited for: 5 -> 4; matrix products, arithmetic and copies ran while one was open for 2% -> 2% of each run, Pallas kernels for 0% -> 0%
where the time goes in v1:
time: 400 us
  waiting for transfers between devices  285 us (71%)
  blocking collectives  61.4 us (15%)
  matrix products  20.4 us (5%)
  between operations  13.2 us (3%)
  local copies, waits for them, and re-layouts  7.15 us (2%)
  starting transfers between devices  6.36 us (2%)
  other arithmetic  6.12 us (2%)
    reduce_scatter x1, waiting for transfers between devices, local(): part = lax.psum_scatter(out, 'y', scatter_dimension=0, tiled=True)  89.4 us
    all_gather x1, waiting for transfers between devices, local(): everyone = lax.all_gather(everyone, 'y', axis=0, tiled=True)  84.2 us
    reduce_scatter x1, waiting for transfers between devices, local(): total = lax.psum_scatter(part, 'z', scatter_dimension=0, tiled=True)  73.6 us
    all_gather x1, blocking collectives, local(): everyone = lax.all_gather(packed, 'z', axis=0, tiled=True)  38.7 us
    reduce_scatter x1, waiting for transfers between devices, local(): lax.psum_scatter(part, ('xh', 'xl'), scatter_dimension=0, tiled=True)  38.1 us
    all_to_all x1, blocking collectives, local(): lax.all_to_all(jnp.stack(lax.psum(1, axis_name=('xh', 'xl')) * [everyone]...  22.7 us
    dot_general x1, matrix products, local(): jnp.dot(hidden, wd, preferred_element_type=jnp.float32).astype(jnp.bfloat16)  13.3 us
  transfers between devices with their start and end apart: 7, of which 4 were waited for; matrix products, arithmetic and copies ran while one was open for 2% of the time, Pallas kernels for 0%

profile of v1, /device:TPU:6, one launch (start us, length us, event | category | flops | bytes accessed | tf_op | source)
XLA Modules:
  0.0 399.9 jit_solution(3073677802018992655)
XLA Ops:
  6.5 0.7 copy-done
  7.2 0.1 constant_dynamic-slice_fusion
  7.3 0.1 copy.20
  7.4 0.8 dynamic-slice_convert_fusion
  8.1 0.1 copy.21
  8.2 0.9 select_reduce_fusion.1
  9.1 0.1 select_reduce_fusion
  9.2 0.8 concatenate.12
  10.1 38.7 %all_gather.6 = bf16[128,2176]{1,0:T(8,128)(2,1)S(1)} all-gather(bf16[8,2176]{1,0:T(8,128)(2,1)S(1)} %concatenate.12), channel_id=1, replica_groups=mesh['xl'=2,'z'=16,'core'=2,'xh'=2,'y'=4] {'z'}, dimensions={0}, use_global_device_ids=true | all-gather | bytes 591872 | tf_op jit(solution)/shard_map/all_gather | solution.py:28
  48.8 0.3 copy.22
  49.1 0.3 stack.2
  49.4 22.7 %all_to_all.5 = bf16[4,128,2176]{1,2,0:T(8,128)(2,1)S(1)} all-to-all(bf16[4,128,2176]{1,2,0:T(8,128)(2,1)S(1)} %stack.2), channel_id=1, replica_groups=mesh['xl'=2,'z'=16,'core'=2,'xh'=2,'y'=4] {'xh','xl'}, dimensions={0} | all-to-all | bytes 4456448 | tf_op jit(solution)/shard_map/all_to_all | solution.py:30
  72.1 2.7 copy.23
  74.8 0.0 all-gather.2.cloned.1.call-update
  74.8 0.0 reduce-scatter.4.cloned.1.call-start
  74.9 1.0 copy-done.1
  75.9 1.9 collective-permute-start.1
  77.8 2.4 collective-permute-start
  80.2 1.9 collective-permute-start.2
  82.2 84.2 %all-gather.2.cloned.1.call-done = bf16[2048,2176]{1,0:T(8,128)(2,1)} async-done(((bf16[512,2176]{1,0:T(8,128)(2,1)}), bf16[2048,2176]{1,0:T(8,128)(2,1)}) %all-gather.2.cloned.1.call-update) | async-done | bytes 8912912 | tf_op jit(solution)/shard_map/all_gather | solution.py:38
  166.4 1.1 slice.9
  167.5 0.7 convert_reduce_fusion.1
  168.2 7.1 %fusion = f32[2048,256]{1,0:T(8,128)} fusion(bf16[2048,2176]{1,0:T(8,128)(2,1)} %all-gather.2.cloned.1.call-done, bf16[2048,128]{1,0:T(8,128)(2,1)S(1)} %collective-permute-done.1, bf16[2048,128]{1,0:T(8,128)(2,1)S(1)} %bitcast.6), kind=kOutput, calls=%fused_computation.1 | convolution fusion | flops 2149580800 | bytes 11534336 | tf_op jit(solution)/shard_map/dot_general | solution.py:54
  175.3 13.3 %convolution_convert_fusion = bf16[2048,2048]{1,0:T(8,128)(2,1)} fusion(f32[2048,256]{1,0:T(8,128)} %fusion, bf16[128,2048]{1,0:T(8,128)(2,1)S(1)} %collective-permute-done.2, bf16[128,2048]{1,0:T(8,128)(2,1)S(1)} %bitcast.8, f32[2048]{0:T(1024)S(1)} %get-tuple-element.6, f32[2048]{0:T(1024)S(1)} %get-tuple-element.5, ...), kind=kOutput, calls=%fused_computation | convolution fusion | flops 4307550208 | bytes 20988160 | tf_op jit(solution)/shard_map/dot_general | solution.py:56
  188.6 0.0 reduce-scatter.4.cloned.1.call-update
  188.6 0.0 reduce-scatter.6.cloned.1.call-start
  188.7 89.4 %reduce-scatter.4.cloned.1.call-done = bf16[512,2048]{1,0:T(8,128)(2,1)} async-done(((bf16[2048,2048]{1,0:T(8,128)(2,1)}), bf16[512,2048]{1,0:T(8,128)(2,1)}) %reduce-scatter.4.cloned.1.call-update) | async-done | bytes 2097168 | tf_op jit(solution)/shard_map/reduce_scatter | solution.py:57
  278.1 0.0 reduce-scatter.8.cloned.1.call-start
  278.1 38.1 %reduce-scatter.6.cloned.1.call-done = bf16[128,2048]{1,0:T(8,128)(2,1)} async-done(((bf16[512,2048]{1,0:T(8,128)(2,1)}), bf16[128,2048]{1,0:T(8,128)(2,1)}) %reduce-scatter.6.cloned.1.call-update) | async-done | bytes 524304 | tf_op jit(solution)/shard_map/reduce_scatter | solution.py:59
  316.2 2.1 convert_element_type.25
  318.4 73.6 %reduce-scatter.8.cloned.1.call-done = f32[8,2048]{1,0:T(8,128)} async-done(((f32[128,2048]{1,0:T(8,128)}), f32[8,2048]{1,0:T(8,128)}) %reduce-scatter.8.cloned.1.call-update) | async-done | bytes 65552 | tf_op jit(solution)/shard_map/reduce_scatter | solution.py:61
  392.0 1.5 convert_element_type.26
  (14 shorter events, 0.1 us)
Async XLA Ops:
  6.5 0.7 copy-start
  6.5 159.9 %all-gather.2.cloned.1.call-start = ((), (), s32[]{:S(2)}) async-start(), calls=%async_computation.4 | async-start | bytes 11141120 | tf_op jit(solution)/shard_map/all_gather | solution.py:38
  74.8 1.0 copy-start.1
  74.8 3.0 copy-start.3
  74.8 5.4 %copy-start.2 = (bf16[1,128,2048]{2,1,0:T(8,128)(2,1)S(1)}, bf16[1,128,2048]{2,1,0:T(8,128)(2,1)}, u32[]{:S(2)}) copy-start(bf16[1,128,2048]{2,1,0:T(8,128)(2,1)} %param.13) | copy-start | bytes 1572868
  74.8 203.2 %reduce-scatter.4.cloned.1.call-start = ((), (), s32[]{:S(2)}) async-start(), calls=%async_computation.5 | async-start | bytes 10485760 | tf_op jit(solution)/shard_map/reduce_scatter | solution.py:57
  75.9 92.4 %collective-permute-start.1 = (bf16[2048,128]{1,0:T(8,128)(2,1)S(1)}, bf16[2048,128]{1,0:T(8,128)(2,1)S(1)}, u32[]{:S(2)}, u32[]{:S(2)}) collective-permute-start(bf16[2048,128]{1,0:T(8,128)(2,1)S(1)} %bitcast.5), channel_id=1, source_target_pairs={{0,8},{8,0},{1,9},{9,1},{2,10},{10,2},{3,11},{11,3},{4,12},{12,4},... | collective-permute-start | bytes 1572872 | tf_op jit(solution)/shard_map/ppermute | solution.py:44
  77.8 97.5 %collective-permute-start = (bf16[2048,128]{1,0:T(8,128)(2,1)S(1)}, bf16[2048,128]{1,0:T(8,128)(2,1)S(1)}, u32[]{:S(2)}, u32[]{:S(2)}) collective-permute-start(bf16[2048,128]{1,0:T(8,128)(2,1)S(1)} %bitcast.9), channel_id=1, source_target_pairs={{0,8},{8,0},{1,9},{9,1},{2,10},{10,2},{3,11},{11,3},{4,12},{12,4},... | collective-permute-start | bytes 1572872 | tf_op jit(solution)/shard_map/ppermute | solution.py:43
  80.2 95.1 %collective-permute-start.2 = (bf16[128,2048]{1,0:T(8,128)(2,1)S(1)}, bf16[128,2048]{1,0:T(8,128)(2,1)S(1)}, u32[]{:S(2)}, u32[]{:S(2)}) collective-permute-start(bf16[128,2048]{1,0:T(8,128)(2,1)S(1)} %bitcast.7), channel_id=1, source_target_pairs={{0,8},{8,0},{1,9},{9,1},{2,10},{10,2},{3,11},{11,3},{4,12},{12,4},... | collective-permute-start | bytes 1572872 | tf_op jit(solution)/shard_map/ppermute | solution.py:45
  188.6 127.6 %reduce-scatter.6.cloned.1.call-start = ((), (), s32[]{:S(2)}) async-start(), calls=%async_computation.6 | async-start | bytes 2621440 | tf_op jit(solution)/shard_map/reduce_scatter | solution.py:59
  278.1 113.9 %reduce-scatter.8.cloned.1.call-start = ((), (), s32[]{:S(2)}) async-start(), calls=%async_computation.7 | async-start | bytes 1114112 | tf_op jit(solution)/shard_map/reduce_scatter | solution.py:61
Sparse Core Ops, SparseCore 0:
  75.0 91.3 all-gather.1
  188.7 89.2 reduce-scatter.3
  280.9 35.2 reduce-scatter.5
  318.9 73.0 reduce-scatter.7
